TPU v7x, 128 devices: a whole 4x4x4 slice. The times are simulated.
128 devices in a mesh: outer: 4 (over x), ctr: 32 (over y, z, core).
Axes of the slice: x: 4, y: 4, z: 4, core: 2. Of those that a mesh axis runs over, the one named last changes fastest.
Arguments:
- amplitudes: float32 [1024, 131072], P(('outer', 'ctr')), may hold values from -24 to 24
- integrals: float32 [4096, 131072], P('outer', 'ctr'), may hold values from -0.015625 to 0.015625
- block_mask: int32 [32, 1024], P('outer', 'ctr'), may hold values 0 or 1
Outputs:
- ladder: float32 [1024, 4096], P('ctr', 'outer')
All inputs are finite; a program needn't handle non-finite values. No bound on the sum of `block_mask` on one device may be relied on, other than what follows from the above.
Results may differ from a plain program's by a relative error of at most 0.000071.
Values sent between devices are 32-bit elements; how exact they have to be, the bound alone decides.
A program may use at most 128 MiB of HBM per device.

v0:
```python
import jax
import jax.numpy as jnp
from jax import lax
from jax.sharding import PartitionSpec as P


def local(amplitudes, integrals, block_mask):
    ab_rows = integrals.shape[0]
    cd_cols = integrals.shape[1]
    ab_blocks = block_mask.shape[0]
    cd_blocks = block_mask.shape[1]
    tile_rows = ab_rows // ab_blocks
    tile_cols = cd_cols // cd_blocks
    mask_f = block_mask.astype(jnp.float32)
    shaped = integrals.reshape(ab_blocks, tile_rows, cd_blocks, tile_cols)
    sparse_v = (shaped * mask_f[:, None, :, None]).reshape(ab_rows, cd_cols)
    local_rows = lax.all_to_all(amplitudes, "ctr", split_axis=1, concat_axis=0, tiled=True)
    partial_terms = lax.dot_general(
        lax.all_gather(local_rows, "outer", axis=0, tiled=True),
        sparse_v,
        (((1,), (1,)), ((), ())),
        precision=lax.Precision.HIGHEST,
        preferred_element_type=jnp.float32,
    )
    summed = lax.psum(partial_terms, "ctr")
    own_rows = summed.shape[0] // lax.axis_size("ctr")
    offset = lax.axis_index("ctr") * own_rows
    result = lax.dynamic_slice_in_dim(summed, offset, own_rows, 0)
    return result


def solution(mesh):
    return jax.shard_map(
        local,
        mesh=mesh,
        in_specs=(P(("outer", "ctr"), None), P("outer", "ctr"), P("outer", "ctr")),
        out_specs=P("ctr", "outer"),
        check_vma=False,
    )
```

profile of v0, /device:TPU:1, one launch (start us, length us, event | category | flops | bytes accessed | tf_op | source)
XLA Modules:
  0.0 415.4 jit_solution(17326440921595013472)
XLA Ops:
  6.5 0.0 all-gather.2.cloned.1.call-start
  6.5 60.3 %all_to_all.19 = f32[8,32,4096]{2,0,1:T(8,128)} all-to-all(f32[8,32,4096]{2,0,1:T(8,128)} %bitcast.20), channel_id=1, replica_groups=mesh['outer'=4,'ctr'=32] {'ctr'}, dimensions={1} | all-to-all | bytes 8388608 | tf_op jit(solution)/shard_map/all_to_all | solution.py:17
  66.8 0.0 all-gather.2.cloned.1.call-update
  66.9 0.0 all-reduce.2.cloned.1.call-start
  66.9 0.7 convert_element_type.3
  67.6 150.8 %all-gather.2.cloned.1.call-done = f32[1024,4096]{1,0:T(8,128)} async-done(((f32[256,4096]{1,0:T(8,128)}), f32[1024,4096]{1,0:T(8,128)}) %all-gather.2.cloned.1.call-update) | async-done | bytes 16777232 | tf_op jit(solution)/shard_map/all_gather | solution.py:19
  218.4 2.2 mul.14
  220.6 72.8 %fusion.2 = f32[1024,1024]{0,1:T(8,128)} fusion(f32[1024,4096]{1,0:T(8,128)} %all-gather.2.cloned.1.call-done, f32[1024,4096]{1,0:T(8,128)} %param.4, f32[128,8,32,128]{3,2,1,0:T(8,128)S(1)} %bitcast.18), kind=kOutput, calls=%fused_computation.3 | convolution fusion | flops 51543801856 | bytes 54525952 | tf_op jit(solution)/shard_map/dot_general | solution.py:18
  293.4 0.0 all-reduce.2.cloned.1.call-update
  293.4 113.1 %all-reduce.2.cloned.1.call-done = f32[1024,1024]{0,1:T(8,128)} async-done(((f32[1024,1024]{0,1:T(8,128)}), f32[1024,1024]{0,1:T(8,128)}) %all-reduce.2.cloned.1.call-update) | async-done | bytes 4194320 | tf_op jit(solution)/shard_map/psum | solution.py:25
  406.5 1.2 constant_dynamic-slice_fusion
  407.7 0.8 copy.4
Async XLA Ops:
  6.5 211.9 %all-gather.2.cloned.1.call-start = ((), (), s32[]{:S(2)}) async-start(), calls=%async_computation.1 | async-start | bytes 20971520 | tf_op jit(solution)/shard_map/all_gather | solution.py:19
  66.9 339.6 %all-reduce.2.cloned.1.call-start = ((), (), s32[]{:S(2)}) async-start(), calls=%async_computation.2 | async-start | bytes 8388608 | tf_op jit(solution)/shard_map/psum | solution.py:25
Sparse Core Ops, SparseCore 0:
  67.0 151.3 all-gather.1
  293.6 112.9 all-reduce.1
where the time goes:
time: 416 us; the launch traced here: 415 us
  waiting for transfers between devices  264 us (63%)
  matrix products  72.8 us (18%)
  blocking collectives  60.3 us (14%)
  between operations  13.4 us (3%)
  local copies, waits for them, and re-layouts  4.28 us (1%)
    all_gather x1, waiting for transfers between devices, local(): lax.all_gather(local_rows, 'outer', axis=0, tiled=True)  151 us
    psum x1, waiting for transfers between devices, local(): summed = lax.psum(partial_terms, 'ctr')  113 us
    dot_general x1, matrix products, local(): lax.dot_general(lax.all_gather(local_rows, 'outer', axis=0, tiled=True),...  72.8 us
    all_to_all x1, blocking collectives, local(): lax.all_to_all(amplitudes, 'ctr', split_axis=1, concat_axis=0, tiled=True)  60.3 us
  transfers between devices with their start and end apart: 2, of which 2 were waited for; matrix products, arithmetic and copies ran while one was open for 0% of the time, Pallas kernels for 0%

commit v1 on v0

--- a/solution.py
+++ b/solution.py
@@ -16,7 +16,9 @@
     sparse_v = (shaped * mask_f[:, None, :, None]).reshape(ab_rows, cd_cols)
     local_rows = lax.all_to_all(amplitudes, "ctr", split_axis=1, concat_axis=0, tiled=True)
     partial_terms = lax.dot_general(
-        lax.all_gather(local_rows, "outer", axis=0, tiled=True),
+        jnp.concatenate(
+            lax.all_to_all(jnp.stack([local_rows] * lax.axis_size("outer")), "outer", 0, 0), axis=0
+        ),
         sparse_v,
         (((1,), (1,)), ((), ())),
         precision=lax.Precision.HIGHEST,

time: 416 us -> 458 us (1.10)
  waiting for transfers between devices: 264 us -> 292 us
  local copies, waits for them, and re-layouts: 4.28 us -> 12.1 us
  starting transfers between devices: 0.04 us -> 7.15 us
    all_to_all x0 -> x1, waiting for transfers between devices: none -> 184 us  [local(): lax.all_to_all(jnp.stack([local_rows] * lax.axis_size('outer')), 'outer',...]
    all_gather x1 -> x0, waiting for transfers between devices: 151 us -> none  [local(): lax.all_gather(local_rows, 'outer', axis=0, tiled=True)]
    another operation x0 -> x1, local copies, waits for them, and re-layouts: none -> 7.81 us  [local(): jnp.stack([local_rows] * lax.axis_size('outer'))]
    all_to_all x0 -> x1, starting transfers between devices: none -> 7.11 us  [local(): lax.all_to_all(jnp.stack([local_rows] * lax.axis_size('outer')), 'outer',...]
    psum x1, waiting for transfers between devices: 113 us -> 108 us  [local(): summed = lax.psum(partial_terms, 'ctr')]
where the time goes in v1:
time: 458 us
  waiting for transfers between devices  292 us (64%)
  matrix products  73 us (16%)
  blocking collectives  60.2 us (13%)
  between operations  13.4 us (3%)
  local copies, waits for them, and re-layouts  12.1 us (3%)
  starting transfers between devices  7.15 us (2%)
    all_to_all x1, waiting for transfers between devices, local(): lax.all_to_all(jnp.stack([local_rows] * lax.axis_size('outer')), 'outer',...  184 us
    psum x1, waiting for transfers between devices, local(): summed = lax.psum(partial_terms, 'ctr')  108 us
    dot_general x1, matrix products, local(): lax.dot_general(jnp.concatenate(lax.all_to_all(jnp.stack([local_rows] * l...  73 us
    all_to_all x1, blocking collectives, local(): lax.all_to_all(amplitudes, 'ctr', split_axis=1, concat_axis=0, tiled=True)  60.2 us
  transfers between devices with their start and end apart: 2, of which 2 were waited for; matrix products, arithmetic and copies ran while one was open for 0% of the time, Pallas kernels for 0%

profile of v1, /device:TPU:1, one launch (start us, length us, event | category | flops | bytes accessed | tf_op | source)
XLA Modules:
  0.0 457.6 jit_solution(3263891169555534720)
XLA Ops:
  6.5 60.2 %all_to_all.21 = f32[8,32,4096]{2,0,1:T(8,128)S(1)} all-to-all(f32[8,32,4096]{2,0,1:T(8,128)} %bitcast.21), channel_id=1, replica_groups=mesh['outer'=4,'ctr'=32] {'ctr'}, dimensions={1} | all-to-all | bytes 8388608 | tf_op jit(solution)/shard_map/all_to_all | solution.py:17
  66.7 7.8 %stack.10 = f32[4,256,4096]{2,1,0:T(8,128)} broadcast(f32[256,4096]{1,0:T(8,128)S(1)} %bitcast.19), dimensions={1,2} | broadcast | bytes 20971520 | tf_op jit(solution)/shard_map/stack | solution.py:20
  74.6 0.0 copy-start
  74.6 7.1 %all-to-all-start.1 = ((f32[4,256,4096]{2,1,0:T(8,128)}), f32[4,256,4096]{2,1,0:T(8,128)}, u32[]{:S(2)}, u32[]{:S(2)}) async-start(f32[4,256,4096]{2,1,0:T(8,128)} %stack.10), calls=%async_computation.1 | async-start | bytes 33554432 | tf_op jit(solution)/shard_map/all_to_all | solution.py:20
  81.7 0.0 all-reduce.2.cloned.1.call-start
  81.7 0.0 copy-done
  81.7 183.6 %all-to-all-done.1 = f32[4,256,4096]{2,1,0:T(8,128)} async-done(((f32[4,256,4096]{2,1,0:T(8,128)}), f32[4,256,4096]{2,1,0:T(8,128)}, u32[]{:S(2)}, u32[]{:S(2)}) %all-to-all-start.1) | async-done | bytes 16777248 | tf_op jit(solution)/shard_map/all_to_all | solution.py:20
  265.3 2.2 mul.14
  267.5 73.0 %fusion.2 = f32[1024,1024]{0,1:T(8,128)} fusion(f32[1024,4096]{1,0:T(8,128)} %bitcast.3, f32[1024,4096]{1,0:T(8,128)} %param.4, f32[128,8,32,128]{3,2,1,0:T(8,128)S(1)} %bitcast.20), kind=kOutput, calls=%fused_computation.3 | convolution fusion | flops 51543801856 | bytes 54525952 | tf_op jit(solution)/shard_map/dot_general | solution.py:18
  340.5 0.0 all-reduce.2.cloned.1.call-update
  340.6 108.1 %all-reduce.2.cloned.1.call-done = f32[1024,1024]{0,1:T(8,128)} async-done(((f32[1024,1024]{0,1:T(8,128)}), f32[1024,1024]{0,1:T(8,128)}) %all-reduce.2.cloned.1.call-update) | async-done | bytes 4194320 | tf_op jit(solution)/shard_map/psum | solution.py:27
  448.7 1.2 constant_dynamic-slice_fusion
  449.9 0.8 copy.4
  (1 shorter events, 0.0 us)
Async XLA Ops:
  74.6 7.2 %copy-start = (s32[8,32]{1,0:T(8,128)S(1)}, s32[8,32]{1,0:T(8,128)}, u32[]{:S(2)}) copy-start(s32[8,32]{1,0:T(8,128)} %param.5) | copy-start | bytes 3076
  74.6 190.8 %all-to-all-start.1 = ((f32[4,256,4096]{2,1,0:T(8,128)}), f32[4,256,4096]{2,1,0:T(8,128)}, u32[]{:S(2)}, u32[]{:S(2)}) async-start(f32[4,256,4096]{2,1,0:T(8,128)} %stack.10), calls=%async_computation.1 | async-start | bytes 33554432 | tf_op jit(solution)/shard_map/all_to_all | solution.py:20
  81.7 367.0 %all-reduce.2.cloned.1.call-start = ((), (), s32[]{:S(2)}) async-start(), calls=%async_computation.2 | async-start | bytes 8388608 | tf_op jit(solution)/shard_map/psum | solution.py:27
Sparse Core Ops, SparseCore 0:
  340.7 107.9 all-reduce.1

commit v2 on v0

--- a/solution.py
+++ b/solution.py
@@ -22,7 +22,9 @@
         precision=lax.Precision.HIGHEST,
         preferred_element_type=jnp.float32,
     )
-    summed = lax.psum(partial_terms, "ctr")
+    summed = partial_terms
+    for hop in (1, 2, 4, 8, 16):
+        summed = summed + lax.ppermute(summed, "ctr", [(dev, dev ^ hop) for dev in range(32)])
     own_rows = summed.shape[0] // lax.axis_size("ctr")
     offset = lax.axis_index("ctr") * own_rows
     result = lax.dynamic_slice_in_dim(summed, offset, own_rows, 0)

time: 416 us -> 687 us (1.65)
  waiting for transfers between devices: 264 us -> 515 us
  other arithmetic: 0.69 us -> 10.3 us
  starting transfers between devices: 0.04 us -> 9.16 us
    ppermute x0 -> x5, waiting for transfers between devices: none -> 364 us  [local(): lax.ppermute(summed, 'ctr', [(dev, dev ^ hop) for dev in range(32)])]
    psum x1 -> x0, waiting for transfers between devices: 113 us -> none  [local(): summed = lax.psum(partial_terms, 'ctr')]
    add x0 -> x5, other arithmetic: none -> 10.3 us  [local(): summed + lax.ppermute(summed, 'ctr', [(dev, dev ^ hop) for dev in range(3...]
    ppermute x0 -> x5, starting transfers between devices: none -> 9.16 us  [local(): lax.ppermute(summed, 'ctr', [(dev, dev ^ hop) for dev in range(32)])]
  transfers between devices with their start and end apart: 2 -> 6, of which waited for: 2 -> 6; matrix products, arithmetic and copies ran while one was open for 0% -> 0% of each run, Pallas kernels for 0% -> 0%
where the time goes in v2:
time: 687 us; the launch traced here: 684 us
  waiting for transfers between devices  515 us (75%)
  matrix products  72.9 us (11%)
  blocking collectives  60.3 us (9%)
  between operations  13.4 us (2%)
  other arithmetic  10.3 us (1%)
  starting transfers between devices  9.16 us (1%)
    ppermute x5, waiting for transfers between devices, local(): lax.ppermute(summed, 'ctr', [(dev, dev ^ hop) for dev in range(32)])  364 us
    all_gather x1, waiting for transfers between devices, local(): lax.all_gather(local_rows, 'outer', axis=0, tiled=True)  151 us
    dot_general x1, matrix products, local(): lax.dot_general(lax.all_gather(local_rows, 'outer', axis=0, tiled=True),...  72.9 us
    all_to_all x1, blocking collectives, local(): lax.all_to_all(amplitudes, 'ctr', split_axis=1, concat_axis=0, tiled=True)  60.3 us
  transfers between devices with their start and end apart: 6, of which 6 were waited for; matrix products, arithmetic and copies ran while one was open for 0% of the time, Pallas kernels for 0%

profile of v2, /device:TPU:1, one launch (start us, length us, event | category | flops | bytes accessed | tf_op | source)
XLA Modules:
  0.0 684.0 jit_solution(11176744206911725345)
XLA Ops:
  6.5 0.0 all-gather.2.cloned.1.call-start
  6.5 60.3 %all_to_all.19 = f32[8,32,4096]{2,0,1:T(8,128)} all-to-all(f32[8,32,4096]{2,0,1:T(8,128)} %bitcast.20), channel_id=1, replica_groups=mesh['outer'=4,'ctr'=32] {'ctr'}, dimensions={1} | all-to-all | bytes 8388608 | tf_op jit(solution)/shard_map/all_to_all | solution.py:17
  66.8 0.0 copy-start
  66.8 0.0 all-gather.2.cloned.1.call-update
  66.9 0.7 copy-done
  67.5 150.9 %all-gather.2.cloned.1.call-done = f32[1024,4096]{1,0:T(8,128)} async-done(((f32[256,4096]{1,0:T(8,128)}), f32[1024,4096]{1,0:T(8,128)}) %all-gather.2.cloned.1.call-update) | async-done | bytes 16777232 | tf_op jit(solution)/shard_map/all_gather | solution.py:19
  218.4 2.2 mul.14
  220.6 72.9 %fusion.2 = f32[1024,1024]{1,0:T(8,128)} fusion(f32[1024,4096]{1,0:T(8,128)} %all-gather.2.cloned.1.call-done, f32[1024,4096]{1,0:T(8,128)} %param.4, f32[128,8,32,128]{3,2,1,0:T(8,128)S(1)} %bitcast.18), kind=kOutput, calls=%fused_computation.3 | convolution fusion | flops 51543801856 | bytes 54525952 | tf_op jit(solution)/shard_map/dot_general | solution.py:18
  293.5 0.8 collective-permute-start
  294.3 7.0 %collective-permute-done = f32[1024,1024]{1,0:T(8,128)S(1)} collective-permute-done((f32[1024,1024]{1,0:T(8,128)}, f32[1024,1024]{1,0:T(8,128)S(1)}, u32[]{:S(2)}, u32[]{:S(2)}) %collective-permute-start) | collective-permute-done | bytes 4194336 | tf_op jit(solution)/shard_map/ppermute | solution.py:27
  301.3 3.1 add.18
  304.4 1.4 collective-permute-start.1
  305.8 90.5 %collective-permute-done.1 = f32[1024,1024]{1,0:T(8,128)S(1)} collective-permute-done((f32[1024,1024]{1,0:T(8,128)S(1)}, f32[1024,1024]{1,0:T(8,128)S(1)}, u32[]{:S(2)}, u32[]{:S(2)}) %collective-permute-start.1) | collective-permute-done | bytes 4194336 | tf_op jit(solution)/shard_map/ppermute | solution.py:27
  396.3 1.4 add.19
  397.6 3.0 collective-permute-start.2
  400.6 89.5 %collective-permute-done.2 = f32[1024,1024]{1,0:T(8,128)S(1)} collective-permute-done((f32[1024,1024]{1,0:T(8,128)S(1)}, f32[1024,1024]{1,0:T(8,128)S(1)}, u32[]{:S(2)}, u32[]{:S(2)}) %collective-permute-start.2) | collective-permute-done | bytes 4194336 | tf_op jit(solution)/shard_map/ppermute | solution.py:27
  490.1 1.4 add.20
  491.5 1.3 collective-permute-start.3
  492.8 88.8 %collective-permute-done.3 = f32[1024,1024]{1,0:T(8,128)S(1)} collective-permute-done((f32[1024,1024]{1,0:T(8,128)S(1)}, f32[1024,1024]{1,0:T(8,128)S(1)}, u32[]{:S(2)}, u32[]{:S(2)}) %collective-permute-start.3) | collective-permute-done | bytes 4194336 | tf_op jit(solution)/shard_map/ppermute | solution.py:27
  581.6 2.9 add.21
  584.5 2.7 collective-permute-start.4
  587.2 88.3 %collective-permute-done.4 = f32[1024,1024]{1,0:T(8,128)} collective-permute-done((f32[1024,1024]{1,0:T(8,128)}, f32[1024,1024]{1,0:T(8,128)}, u32[]{:S(2)}, u32[]{:S(2)}) %collective-permute-start.4) | collective-permute-done | bytes 4194336 | tf_op jit(solution)/shard_map/ppermute | solution.py:27
  675.5 1.6 dynamic-slice_add_fusion
  (1 shorter events, 0.0 us)
Async XLA Ops:
  6.5 211.9 %all-gather.2.cloned.1.call-start = ((), (), s32[]{:S(2)}) async-start(), calls=%async_computation.1 | async-start | bytes 20971520 | tf_op jit(solution)/shard_map/all_gather | solution.py:19
  66.8 0.7 copy-start
  293.5 7.8 %collective-permute-start = (f32[1024,1024]{1,0:T(8,128)}, f32[1024,1024]{1,0:T(8,128)S(1)}, u32[]{:S(2)}, u32[]{:S(2)}) collective-permute-start(f32[1024,1024]{1,0:T(8,128)} %fusion.2), channel_id=1, source_target_pairs={{0,1},{1,0},{2,3},{3,2},{4,5},{5,4},{6,7},{7,6},{8,9},{9,8},{10,11... | collective-permute-start | bytes 12582920 | tf_op jit(solution)/shard_map/ppermute | solution.py:27
  304.4 91.8 %collective-permute-start.1 = (f32[1024,1024]{1,0:T(8,128)S(1)}, f32[1024,1024]{1,0:T(8,128)S(1)}, u32[]{:S(2)}, u32[]{:S(2)}) collective-permute-start(f32[1024,1024]{1,0:T(8,128)S(1)} %add.18), channel_id=1, source_target_pairs={{0,2},{1,3},{2,0},{3,1},{4,6},{5,7},{6,4},{7,5},{8,10},{9,11},{10,... | collective-permute-start | bytes 12582920 | tf_op jit(solution)/shard_map/ppermute | solution.py:27
  397.6 92.5 %collective-permute-start.2 = (f32[1024,1024]{1,0:T(8,128)S(1)}, f32[1024,1024]{1,0:T(8,128)S(1)}, u32[]{:S(2)}, u32[]{:S(2)}) collective-permute-start(f32[1024,1024]{1,0:T(8,128)S(1)} %add.19), channel_id=1, source_target_pairs={{0,4},{1,5},{2,6},{3,7},{4,0},{5,1},{6,2},{7,3},{8,12},{9,13},{10,... | collective-permute-start | bytes 12582920 | tf_op jit(solution)/shard_map/ppermute | solution.py:27
  491.5 90.1 %collective-permute-start.3 = (f32[1024,1024]{1,0:T(8,128)S(1)}, f32[1024,1024]{1,0:T(8,128)S(1)}, u32[]{:S(2)}, u32[]{:S(2)}) collective-permute-start(f32[1024,1024]{1,0:T(8,128)S(1)} %add.20), channel_id=1, source_target_pairs={{0,8},{1,9},{2,10},{3,11},{4,12},{5,13},{6,14},{7,15},{8,0},{9,1},... | collective-permute-start | bytes 12582920 | tf_op jit(solution)/shard_map/ppermute | solution.py:27
  584.5 91.0 %collective-permute-start.4 = (f32[1024,1024]{1,0:T(8,128)}, f32[1024,1024]{1,0:T(8,128)}, u32[]{:S(2)}, u32[]{:S(2)}) collective-permute-start(f32[1024,1024]{1,0:T(8,128)} %add.21), channel_id=1, source_target_pairs={{0,16},{1,17},{2,18},{3,19},{4,20},{5,21},{6,22},{7,23},{8,24},{9,... | collective-permute-start | bytes 12582920 | tf_op jit(solution)/shard_map/ppermute | solution.py:27
Sparse Core Ops, SparseCore 0:
  67.0 151.3 all-gather.1
